TPU v7x, 32 devices: a whole 2x2x4 slice. The times are simulated.
32 devices in a mesh: freq: 16 (over z, y, core), rows: 2 (over x).
Axes of the slice: x: 2, y: 2, z: 4, core: 2. Of those that a mesh axis runs over, the one named last changes fastest.
Arguments:
- kernel: bfloat16 [2, 128, 2048, 2048], P(None, 'freq', 'rows'), may hold values from -0.25 to 0.25
- tile_mask: int32 [128, 16, 16], P('freq', 'rows'), may hold values 0 or 1
- direct: float32 [2048, 128, 512], P(('rows', 'freq')), may hold values from -6 to 6
- onsets: int32 [2048, 128], P(('rows', 'freq')), may hold values from 64 to 447
Outputs:
- focusing: float32 [2048, 128, 512], P(('rows', 'freq'))
Inputs may be any that keep to these rules, and one draw needn't show every extreme that they name: `tile_mask`: 0 drops a tile, 1 keeps it.
All inputs are finite; a program needn't handle non-finite values. No bound on the sum of `tile_mask` on one device may be relied on, other than what follows from the above.
Results may differ from a plain program's by a relative error of at most 0.0026.
Values may be sent and summed in bfloat16 or wider, within the bound.
No kernel may reach another device: no remote copies, remote signals or barrier semaphores. Data moves between devices by JAX's collectives and lax.ppermute only.
A program may use at most 320 MiB of HBM per device.

v0:
```python
import math
import jax
import jax.numpy as jnp
from jax import lax
from jax.sharding import PartitionSpec as P

NF = 128
NT = 512
TILE = 128
ITERS = 2


def phase_table():
    freq_ids = jnp.arange(NF, dtype=jnp.int32) + 1
    time_ids = jnp.arange(NT, dtype=jnp.int32)
    phase_ids = freq_ids[:, None] * time_ids[None, :] % NT
    angles = phase_ids.astype(jnp.float32) * (2.0 * math.pi / NT)
    norm_scale = math.sqrt(2.0 / NT)
    return jnp.stack([jnp.cos(angles), -jnp.sin(angles)]) * norm_scale


def multiply(weights, fields):
    real_real = jnp.einsum(
        "fmk,fkp->fmp", weights[0], fields[0], preferred_element_type=jnp.float32
    )
    imag_imag = jnp.einsum(
        "fmk,fkp->fmp", weights[1], fields[1], preferred_element_type=jnp.float32
    )
    real_imag = jnp.einsum(
        "fmk,fkp->fmp", weights[0], fields[1], preferred_element_type=jnp.float32
    )
    imag_real = jnp.einsum(
        "fmk,fkp->fmp", weights[1], fields[0], preferred_element_type=jnp.float32
    )
    return jnp.stack([real_real - imag_imag, real_imag + imag_real])


def products(masked, fields):
    return multiply(masked, lax.all_gather(fields, "rows", axis=2, tiled=True))


def forward(masked, fields, direct, window, dft_table):
    bands = products(masked, fields).astype(jnp.bfloat16)
    traces = lax.all_to_all(bands, "freq", split_axis=2, concat_axis=1, tiled=True)
    series = jnp.einsum(
        "kjrp,kjt->rpt", traces.astype(jnp.float32), dft_table, precision=lax.Precision.HIGHEST
    )
    return direct - jnp.where(window, series, 0.0)


def to_bands(focusing, dft_table):
    spectra = jnp.einsum(
        "rpt,kjt->kjrp", focusing, dft_table, precision=lax.Precision.HIGHEST
    ).astype(jnp.bfloat16)
    bands = lax.all_to_all(spectra, "freq", split_axis=1, concat_axis=2, tiled=True)
    return bands


def local(kernel, tile_mask, direct, onsets):
    dft_table = phase_table()
    full_mask = jnp.repeat(jnp.repeat(tile_mask, TILE, axis=1), TILE, axis=2).astype(jnp.bfloat16)
    masked = kernel * full_mask[None]
    time_ids = jnp.arange(NT, dtype=jnp.int32)
    window = time_ids[None, None, :] < onsets[:, :, None]
    fields = to_bands(direct, dft_table)
    focusing = direct
    for iteration in range(ITERS):
        focusing = forward(masked, fields, direct, window, dft_table)
        if iteration + 1 < ITERS:
            fields = to_bands(focusing, dft_table)
    return focusing


def solution(mesh):
    return jax.shard_map(
        local,
        mesh=mesh,
        in_specs=(
            P(None, "freq", "rows", None),
            P("freq", "rows", None),
            P(("rows", "freq"), None, None),
            P(("rows", "freq"), None),
        ),
        out_specs=P(("rows", "freq"), None, None),
        check_vma=False,
    )
```

profile of v0, /device:TPU:1, one launch (start us, length us, event | category | flops | bytes accessed | tf_op | source)
XLA Modules:
  0.0 853.0 jit_solution(786638177936812693)
XLA Ops:
  8.4 16.9 %fusion.20 = bf16[2,128,64,128]{3,1,2,0:T(8,128)(2,1)S(1)} fusion(f32[64,128,512]{2,1,0:T(8,128)} %param.6, f32[1,128,512]{2,1,0:T(8,128)S(1)} %get-tuple-element.6, f32[1,128,512]{2,1,0:T(8,128)S(1)} %get-tuple-element.5), kind=kOutput, calls=%fused_computation.35 | convolution fusion | flops 12887261184 | bytes 21495808 | tf_op jit(solution)/shard_map/rpt,kjt->kjrp/dot_general | solution.py:52
  25.4 4.7 copy.21
  30.1 7.3 all-to-all-start
  37.8 21.0 %broadcast_in_dim.17 = bf16[8,1024,16,128]{3,2,1,0:T(8,128)(2,1)} broadcast(bf16[8,1024,16]{2,1,0:T(8,128)(2,1)S(1)} %bitcast.116), dimensions={0,1,2} | broadcast | bytes 33816576 | tf_op jit(solution)/shard_map/broadcast_in_dim | solution.py:61
  58.7 49.3 %convert_element_type.43 = bf16[8,1024,2048]{2,1,0:T(8,128)(2,1)} reshape(bf16[8,1024,16,128]{3,2,1,0:T(8,128)(2,1)} %broadcast_in_dim.17) | data formatting | bytes 67108864 | tf_op jit(solution)/shard_map/convert_element_type | solution.py:61
  108.0 7.5 all-to-all-done
  115.6 5.6 copy.22
  121.4 56.1 %broadcast_multiply_fusion = bf16[2,8,1024,2048]{3,2,1,0:T(8,128)(2,1)} fusion(bf16[2,8,1024,2048]{3,2,1,0:T(8,128)(2,1)} %param.4, bf16[8,1024,2048]{2,1,0:T(8,128)(2,1)} %convert_element_type.43), kind=kLoop, calls=%fused_computation.2 | loop fusion | flops 33554432 | bytes 167772160 | tf_op jit(solution)/shard_map/mul | solution.py:62
  177.6 61.4 %all-gather.3.cloned.1.call-done = bf16[2,8,2048,128]{3,2,1,0:T(8,128)(2,1)} async-done(((bf16[2,8,1024,128]{3,2,1,0:T(8,128)(2,1)}), bf16[2,8,2048,128]{3,2,1,0:T(8,128)(2,1)}) %all-gather.3.cloned.1.call-update) | async-done | bytes 8388624 | tf_op jit(solution)/shard_map/all_gather | solution.py:39
  239.0 17.6 %fusion.2 = f32[8,1024,128]{2,1,0:T(8,128)} fusion(bf16[2,8,1024,2048]{3,2,1,0:T(8,128)(2,1)} %broadcast_multiply_fusion, bf16[2,8,2048,128]{3,2,1,0:T(8,128)(2,1)} %all-gather.3.cloned.1.call-done), kind=kOutput, calls=%fused_computation.5 | convolution fusion | flops 4294967296 | bytes 41943040 | tf_op jit(solution)/shard_map/fmk,fkp->fmp/dot_general | solution.py:29
  256.6 17.7 %fusion.3 = f32[8,1024,128]{2,1,0:T(8,128)} fusion(bf16[2,8,1024,2048]{3,2,1,0:T(8,128)(2,1)} %broadcast_multiply_fusion, bf16[2,8,2048,128]{3,2,1,0:T(8,128)(2,1)} %all-gather.3.cloned.1.call-done), kind=kOutput, calls=%fused_computation.6 | convolution fusion | flops 4294967296 | bytes 41943040 | tf_op jit(solution)/shard_map/fmk,fkp->fmp/dot_general | solution.py:23
  274.2 16.7 %fusion.27 = bf16[1,8,1024,128]{3,2,1,0:T(8,128)(2,1)S(1)} fusion(f32[8,1024,128]{2,1,0:T(8,128)} %fusion.2, bf16[2,8,2048,128]{3,2,1,0:T(8,128)(2,1)} %all-gather.3.cloned.1.call-done, bf16[2,8,1024,2048]{3,2,1,0:T(8,128)(2,1)} %broadcast_multiply_fusion), kind=kOutput, calls=%fused_computation.38 | convolution fusion | flops 4297064448 | bytes 44040192 | tf_op jit(solution)/shard_map/fmk,fkp->fmp/dot_general | solution.py:32
  290.9 16.9 %fusion.26 = bf16[1,8,1024,128]{3,2,1,0:T(8,128)(2,1)S(1)} fusion(f32[8,1024,128]{2,1,0:T(8,128)} %fusion.3, bf16[2,8,2048,128]{3,2,1,0:T(8,128)(2,1)} %all-gather.3.cloned.1.call-done, bf16[2,8,1024,2048]{3,2,1,0:T(8,128)(2,1)} %broadcast_multiply_fusion), kind=kOutput, calls=%fused_computation.37 | convolution fusion | flops 4297064448 | bytes 44040192 | tf_op jit(solution)/shard_map/fmk,fkp->fmp/dot_general | solution.py:26
  310.9 99.4 %all_to_all.72 = bf16[2,8,1024,128]{3,1,0,2:T(8,128)(2,1)S(1)} all-to-all(bf16[2,8,1024,128]{3,1,0,2:T(8,128)(2,1)S(1)} %copy.23), channel_id=1, replica_groups=mesh['freq'=16,'rows'=2] {'freq'}, dimensions={2} | all-to-all | bytes 8388608 | tf_op jit(solution)/shard_map/all_to_all | solution.py:44
  411.5 17.6 %fusion.18 = f32[64,128,512,1]{2,1,3,0:T(8,128)} fusion(bf16[2,128,64,128]{3,2,1,0:T(8,128)(2,1)S(1)} %bitcast.109, f32[1,128,512]{2,1,0:T(8,128)S(1)} %copy-done.3, f32[1,128,512]{2,1,0:T(8,128)S(1)} %copy-done.1), kind=kOutput, calls=%fused_computation.29 | convolution fusion | flops 12885164032 | bytes 21495808 | tf_op jit(solution)/shard_map/kjrp,kjt->rpt/dot_general | solution.py:45
  429.2 18.9 %fusion.23 = bf16[2,128,64,128]{3,1,2,0:T(8,128)(2,1)S(1)} fusion(f32[64,128,512]{2,1,0:T(8,128)S(1)} %bitcast.108, f32[64,128,512,1]{2,1,3,0:T(8,128)} %fusion.18, s32[64,128]{1,0:T(8,128)S(1)} %copy-done.4, f32[1,128,512]{2,1,0:T(8,128)S(1)} %copy-done.3, f32[1,128,512]{2,1,0:T(8,128)S(1)} %copy-done.1), kind=kOutput, calls=%fused_computation.36 | convolution fusion | flops 12899844096 | bytes 38305792 | tf_op jit(solution)/shard_map/rpt,kjt->kjrp/dot_general | solution.py:52
  450.8 97.4 %all_to_all.73 = bf16[2,128,64,128]{3,2,0,1:T(8,128)(2,1)S(1)} all-to-all(bf16[2,128,64,128]{3,2,0,1:T(8,128)(2,1)S(1)} %copy.27), channel_id=1, replica_groups=mesh['freq'=16,'rows'=2] {'freq'}, dimensions={1} | all-to-all | bytes 8388608 | tf_op jit(solution)/shard_map/all_to_all | solution.py:55
  551.2 102.6 %all-gather.5.cloned.1.call-done = bf16[2,8,2048,128]{3,2,1,0:T(8,128)(2,1)} async-done(((bf16[2,8,1024,128]{3,2,1,0:T(8,128)(2,1)}), bf16[2,8,2048,128]{3,2,1,0:T(8,128)(2,1)}) %all-gather.5.cloned.1.call-update) | async-done | bytes 8388624 | tf_op jit(solution)/shard_map/all_gather | solution.py:39
  653.8 17.7 %fusion = f32[8,1024,128]{2,1,0:T(8,128)} fusion(bf16[2,8,1024,2048]{3,2,1,0:T(8,128)(2,1)} %broadcast_multiply_fusion, bf16[2,8,2048,128]{3,2,1,0:T(8,128)(2,1)} %all-gather.5.cloned.1.call-done), kind=kOutput, calls=%fused_computation.3 | convolution fusion | flops 4294967296 | bytes 41943040 | tf_op jit(solution)/shard_map/fmk,fkp->fmp/dot_general | solution.py:29
  671.5 17.6 %fusion.1 = f32[8,1024,128]{2,1,0:T(8,128)} fusion(bf16[2,8,1024,2048]{3,2,1,0:T(8,128)(2,1)} %broadcast_multiply_fusion, bf16[2,8,2048,128]{3,2,1,0:T(8,128)(2,1)} %all-gather.5.cloned.1.call-done), kind=kOutput, calls=%fused_computation.4 | convolution fusion | flops 4294967296 | bytes 41943040 | tf_op jit(solution)/shard_map/fmk,fkp->fmp/dot_general | solution.py:23
  689.1 16.7 %fusion.29 = bf16[1,8,1024,128]{3,2,1,0:T(8,128)(2,1)S(1)} fusion(f32[8,1024,128]{2,1,0:T(8,128)} %fusion, bf16[2,8,2048,128]{3,2,1,0:T(8,128)(2,1)} %all-gather.5.cloned.1.call-done, bf16[2,8,1024,2048]{3,2,1,0:T(8,128)(2,1)} %broadcast_multiply_fusion), kind=kOutput, calls=%fused_computation.40 | convolution fusion | flops 4297064448 | bytes 44040192 | tf_op jit(solution)/shard_map/fmk,fkp->fmp/dot_general | solution.py:32
  705.7 16.9 %fusion.28 = bf16[1,8,1024,128]{3,2,1,0:T(8,128)(2,1)S(1)} fusion(f32[8,1024,128]{2,1,0:T(8,128)} %fusion.1, bf16[2,8,2048,128]{3,2,1,0:T(8,128)(2,1)} %all-gather.5.cloned.1.call-done, bf16[2,8,1024,2048]{3,2,1,0:T(8,128)(2,1)} %broadcast_multiply_fusion), kind=kOutput, calls=%fused_computation.39 | convolution fusion | flops 4297064448 | bytes 44040192 | tf_op jit(solution)/shard_map/fmk,fkp->fmp/dot_general | solution.py:26
  725.8 98.8 %all_to_all.74 = bf16[2,8,1024,128]{3,1,0,2:T(8,128)(2,1)S(1)} all-to-all(bf16[2,8,1024,128]{3,1,0,2:T(8,128)(2,1)S(1)} %copy.29), channel_id=1, replica_groups=mesh['freq'=16,'rows'=2] {'freq'}, dimensions={2} | all-to-all | bytes 8388608 | tf_op jit(solution)/shard_map/all_to_all | solution.py:44
  825.7 20.1 %fusion.8 = f32[64,128,512]{2,1,0:T(8,128)} fusion(f32[64,128,512]{2,1,0:T(8,128)} %param.6, s32[64,128]{1,0:T(8,128)S(1)} %copy-done.4, bf16[2,128,64,128]{3,2,1,0:T(8,128)(2,1)S(1)} %bitcast.115, f32[1,128,512]{2,1,0:T(8,128)S(1)} %copy-done.3, f32[1,128,512]{2,1,0:T(8,128)S(1)} %copy-done.1), kind=kOutput, calls=%fused_computation.12 | convolution fusion | flops 12897746944 | bytes 38305792 | tf_op jit(solution)/shard_map/kjrp,kjt->rpt/dot_general | solution.py:45
  (37 shorter events, 16.5 us)
Async XLA Ops:
  7.6 0.7 copy-start
  7.7 0.8 copy-start.2
  25.4 12.1 %copy-start.5 = (s32[8,8,16]{2,1,0:T(8,128)S(1)}, s32[8,8,16]{2,1,0:T(8,128)}, u32[]{:S(2)}) copy-start(s32[8,8,16]{2,1,0:T(8,128)} %param.5) | copy-start | bytes 12292
  30.1 85.5 %all-to-all-start = ((bf16[2,128,64,128]{3,2,0,1:T(8,128)(2,1)}), bf16[2,128,64,128]{3,2,0,1:T(8,128)(2,1)}, u32[]{:S(2)}, u32[]{:S(2)}) async-start(bf16[2,128,64,128]{3,2,0,1:T(8,128)(2,1)} %copy.21), calls=%async_computation | async-start | bytes 8388608 | tf_op jit(solution)/shard_map/all_to_all | solution.py:55
  37.4 201.6 %all-gather.3.cloned.1.call-start = ((), (), s32[]{:S(2)}) async-start(), calls=%async_computation.4 | async-start | bytes 12582912 | tf_op jit(solution)/shard_map/all_gather | solution.py:39
  121.2 532.7 %all-gather.5.cloned.1.call-start = ((), (), s32[]{:S(2)}) async-start(), calls=%async_computation.5 | async-start | bytes 12582912 | tf_op jit(solution)/shard_map/all_gather | solution.py:39
  310.9 100.5 %copy-start.1 = (f32[1,128,512]{2,1,0:T(8,128)S(1)}, f32[1,128,512]{2,1,0:T(8,128)}, u32[]{:S(2)}) copy-start(f32[1,128,512]{2,1,0:T(8,128)} %copy-done) | copy-start | bytes 786436
  310.9 100.5 %copy-start.3 = (f32[1,128,512]{2,1,0:T(8,128)S(1)}, f32[1,128,512]{2,1,0:T(8,128)}, u32[]{:S(2)}) copy-start(f32[1,128,512]{2,1,0:T(8,128)} %copy-done.2) | copy-start | bytes 786436
  410.4 18.8 %slice-start = ((s8[16777216]{0:T(1024)(128)(4,1)}), s8[4194304]{0:T(1024)(128)(4,1)S(1)}, s32[]{:S(2)}) async-start(s8[16777216]{0:T(1024)(128)(4,1)} %bitcast.107), calls=%async_computation.6 | async-start | bytes 8388608
  411.5 17.7 %slice-start.1 = ((s8[16777216]{0:T(1024)(128)(4,1)}), s8[4194304]{0:T(1024)(128)(4,1)S(1)}, s32[]{:S(2)}) async-start(s8[16777216]{0:T(1024)(128)(4,1)} %bitcast.107), calls=%async_computation.7 | async-start | bytes 8388608
  411.5 17.7 %slice-start.2 = ((s8[16777216]{0:T(1024)(128)(4,1)}), s8[4194304]{0:T(1024)(128)(4,1)S(1)}, s32[]{:S(2)}) async-start(s8[16777216]{0:T(1024)(128)(4,1)} %bitcast.107), calls=%async_computation.8 | async-start | bytes 8388608
  411.5 17.7 %slice-start.3 = ((s8[16777216]{0:T(1024)(128)(4,1)}), s8[4194304]{0:T(1024)(128)(4,1)S(1)}, s32[]{:S(2)}) async-start(s8[16777216]{0:T(1024)(128)(4,1)} %bitcast.107), calls=%async_computation.9 | async-start | bytes 8388608
  411.5 17.7 %copy-start.4 = (s32[64,128]{1,0:T(8,128)S(1)}, s32[64,128]{1,0:T(8,128)}, u32[]{:S(2)}) copy-start(s32[64,128]{1,0:T(8,128)} %param.7) | copy-start | bytes 98308
Sparse Core Ops, SparseCore 0:
  121.3 117.6 all-gather.2
  551.4 102.4 all-gather.4
where the time goes:
time: 862 us; the launch traced here: 853 us
  blocking collectives  296 us (34%)
  matrix products  211 us (24%)
  waiting for transfers between devices  172 us (20%)
  local copies, waits for them, and re-layouts  94.9 us (11%)
  other arithmetic  58 us (7%)
  between operations  14.1 us (2%)
    all_to_all x2, blocking collectives, forward(): lax.all_to_all(bands, 'freq', split_axis=2, concat_axis=1, tiled=True)  198 us
    all_gather x2, waiting for transfers between devices, products(): return multiply(masked, lax.all_gather(fields, 'rows', axis=2, tiled=True))  164 us
    all_to_all x1, blocking collectives, to_bands(): lax.all_to_all(spectra, 'freq', split_axis=1, concat_axis=2, tiled=True)  97.4 us
    mul x1, other arithmetic, local(): masked = kernel * full_mask[None]  56.1 us
    convert_element_type x1, local copies, waits for them, and re-layouts, local(): jnp.repeat(jnp.repeat(tile_mask, TILE, axis=1), TILE, axis=2)  49.3 us
    dot_general x2, matrix products, forward(): jnp.einsum('kjrp,kjt->rpt', traces.astype(jnp.float32), dft_table, precis...  37.7 us
    dot_general x2, matrix products, to_bands(): jnp.einsum('rpt,kjt->kjrp', focusing, dft_table, precision=lax.Precision....  35.8 us
    dot_general x2, matrix products, multiply(): jnp.einsum('fmk,fkp->fmp', weights[0], fields[1], preferred_element_type=...  35.2 us
  transfers between devices with their start and end apart: 3, of which 3 were waited for; matrix products, arithmetic and copies ran while one was open for 15% of the time, Pallas kernels for 0%

commit v1 on v0

--- a/solution.py
+++ b/solution.py
@@ -3,6 +3,7 @@
 import jax.numpy as jnp
 from jax import lax
 from jax.sharding import PartitionSpec as P
+from jax.lax import axis_index, axis_size, ppermute
 
 NF = 128
 NT = 512
@@ -52,7 +53,21 @@
     spectra = jnp.einsum(
         "rpt,kjt->kjrp", focusing, dft_table, precision=lax.Precision.HIGHEST
     ).astype(jnp.bfloat16)
-    bands = lax.all_to_all(spectra, "freq", split_axis=1, concat_axis=2, tiled=True)
+    near = axis_size("freq")
+    z1 = axis_index("freq")
+    carry, carry_in = (near, z1)
+    current_block = spectra.shape[1] // carry
+    all_values = jnp.roll(spectra, -carry_in * current_block, 1)
+    x_now = lax.slice_in_dim(all_values, 0, current_block, axis=1)
+    vals = [x_now]
+    for jj in range(1, carry):
+        g_now = lax.slice_in_dim(all_values, jj * current_block, (jj + 1) * current_block, axis=1)
+        big = ppermute(
+            g_now, axis_name="freq", perm=[(pp, (pp + jj) % carry) for pp in range(carry)]
+        )
+        vals.append(big)
+    z2 = jnp.concatenate(vals[::-1], 2)
+    bands = jnp.roll(z2, (carry_in + 1) * vals[0].shape[2], 2)
     return bands
 
 

time: 862 us -> 969 us (1.12)
  blocking collectives: 296 us -> 198 us
  waiting for transfers between devices: 172 us -> 267 us
  starting transfers between devices: 7.63 us -> 67.4 us
  other arithmetic: 58 us -> 97.6 us
    ppermute x0 -> x30, waiting for transfers between devices: none -> 105 us  [to_bands(): ppermute(g_now, axis_name='freq', perm=[(pp, (pp + jj) % carry) for pp in...]
    all_to_all x1 -> x0, blocking collectives: 97.4 us -> none  [to_bands(): lax.all_to_all(spectra, 'freq', split_axis=1, concat_axis=2, tiled=True)]
    ppermute x0 -> x30, starting transfers between devices: none -> 67.1 us  [to_bands(): ppermute(g_now, axis_name='freq', perm=[(pp, (pp + jj) % carry) for pp in...]
    concatenate x0 -> x4, other arithmetic: none -> 36.5 us  [the longest x2 32.1 us: to_bands(): bands = jnp.roll(z2, (carry_in + 1) * vals[0].shape[2], 2)]
    squeeze x0 -> x2, local copies, waits for them, and re-layouts: none -> 11.9 us  [multiply(): fields[0]]
  transfers between devices with their start and end apart: 3 -> 32, of which waited for: 3 -> 13; matrix products, arithmetic and copies ran while one was open for 15% -> 14% of each run, Pallas kernels for 0% -> 0%
where the time goes in v1:
time: 969 us; the launch traced here: 960 us
  waiting for transfers between devices  267 us (28%)
  matrix products  215 us (22%)
  blocking collectives  198 us (20%)
  local copies, waits for them, and re-layouts  102 us (11%)
  other arithmetic  97.6 us (10%)
  starting transfers between devices  67.4 us (7%)
  between operations  14.2 us (1%)
    all_to_all x2, blocking collectives, forward(): lax.all_to_all(bands, 'freq', split_axis=2, concat_axis=1, tiled=True)  198 us
    all_gather x2, waiting for transfers between devices, products(): return multiply(masked, lax.all_gather(fields, 'rows', axis=2, tiled=True))  162 us
    ppermute x30, waiting for transfers between devices, to_bands(): ppermute(g_now, axis_name='freq', perm=[(pp, (pp + jj) % carry) for pp in...  105 us
    ppermute x30, starting transfers between devices, to_bands(): ppermute(g_now, axis_name='freq', perm=[(pp, (pp + jj) % carry) for pp in...  67.1 us
    mul x1, other arithmetic, local(): masked = kernel * full_mask[None]  56 us
    convert_element_type x1, local copies, waits for them, and re-layouts, local(): jnp.repeat(jnp.repeat(tile_mask, TILE, axis=1), TILE, axis=2)  49.3 us
    dot_general x2, matrix products, forward(): jnp.einsum('kjrp,kjt->rpt', traces.astype(jnp.float32), dft_table, precis...  37.7 us
    dot_general x2, matrix products, to_bands(): jnp.einsum('rpt,kjt->kjrp', focusing, dft_table, precision=lax.Precision....  36 us
  transfers between devices with their start and end apart: 32, of which 13 were waited for; matrix products, arithmetic and copies ran while one was open for 14% of the time, Pallas kernels for 0%

profile of v1, /device:TPU:1, one launch (start us, length us, event | category | flops | bytes accessed | tf_op | source)
XLA Modules:
  0.0 960.1 jit_solution(2553814570183866566)
XLA Ops:
  7.7 17.1 %fusion.32 = bf16[2,128,64,128]{3,1,2,0:T(8,128)(2,1)S(1)} fusion(f32[64,128,512]{2,1,0:T(8,128)} %param.10, f32[1,128,512]{2,1,0:T(8,128)S(1)} %get-tuple-element.42, f32[1,128,512]{2,1,0:T(8,128)S(1)} %get-tuple-element.41), kind=kOutput, calls=%fused_computation.55 | convolution fusion | flops 12887261184 | bytes 21495808 | tf_op jit(solution)/shard_map/rpt,kjt->kjrp/dot_general | solution.py:53
  38.4 20.9 %broadcast_in_dim.17 = bf16[8,1024,16,128]{3,2,1,0:T(8,128)(2,1)} broadcast(bf16[8,1024,16]{2,1,0:T(8,128)(2,1)S(1)} %bitcast.89), dimensions={0,1,2} | broadcast | bytes 33816576 | tf_op jit(solution)/shard_map/broadcast_in_dim | solution.py:76
  59.4 49.3 %convert_element_type.43 = bf16[8,1024,2048]{2,1,0:T(8,128)(2,1)} reshape(bf16[8,1024,16,128]{3,2,1,0:T(8,128)(2,1)} %broadcast_in_dim.17) | data formatting | bytes 67108864 | tf_op jit(solution)/shard_map/convert_element_type | solution.py:76
  126.3 32.0 %collective-permute-done.6 = bf16[2,8,64,128]{3,1,2,0:T(8,128)(2,1)S(1)} collective-permute-done((bf16[2,8,64,128]{3,1,2,0:T(8,128)(2,1)S(1)}, bf16[2,8,64,128]{3,1,2,0:T(8,128)(2,1)S(1)}, u32[]{:S(2)}, u32[]{:S(2)}) %collective-permute-start.6) | collective-permute-done | bytes 262176 | tf_op jit(solution)/shard_map/ppermute | solution.py:65
  187.5 15.9 %fusion.19 = bf16[2,8,1024,128]{3,1,2,0:T(8,128)(2,1)} fusion(s32[]{:T(128)S(6)} %select_n.53, bf16[2,8,1024,128]{3,1,2,0:T(8,128)(2,1)S(1)} %slice_dynamic-update-slice_fusion.1), kind=kLoop, calls=%fused_computation.32 | loop fusion | flops 2097152 | bytes 8388612 | tf_op jit(solution)/shard_map/jit(_roll_dynamic)/concatenate | solution.py:70
  203.7 56.0 %broadcast_multiply_fusion = bf16[2,8,1024,2048]{3,2,1,0:T(8,128)(2,1)} fusion(bf16[2,8,1024,2048]{3,2,1,0:T(8,128)(2,1)} %param.8, bf16[8,1024,2048]{2,1,0:T(8,128)(2,1)} %convert_element_type.43), kind=kLoop, calls=%fused_computation.2 | loop fusion | flops 33554432 | bytes 167772160 | tf_op jit(solution)/shard_map/mul | solution.py:77
  259.7 51.0 %all-gather.3.cloned.1.call-done = bf16[2,8,2048,128]{3,1,2,0:T(8,128)(2,1)} async-done(((bf16[2,8,1024,128]{3,1,2,0:T(8,128)(2,1)}), bf16[2,8,2048,128]{3,1,2,0:T(8,128)(2,1)}) %all-gather.3.cloned.1.call-update) | async-done | bytes 8388624 | tf_op jit(solution)/shard_map/all_gather | solution.py:40
  316.5 17.6 %fusion.2 = f32[8,1024,128]{2,1,0:T(8,128)} fusion(bf16[2,8,1024,2048]{3,2,1,0:T(8,128)(2,1)} %broadcast_multiply_fusion, bf16[8,2048,128]{2,0,1:T(8,128)(2,1)} %get-tuple-element.10), kind=kOutput, calls=%fused_computation.5 | convolution fusion | flops 4294967296 | bytes 41943040 | tf_op jit(solution)/shard_map/fmk,fkp->fmp/dot_general | solution.py:30
  334.1 17.6 %fusion.3 = f32[8,1024,128]{2,1,0:T(8,128)} fusion(bf16[2,8,1024,2048]{3,2,1,0:T(8,128)(2,1)} %broadcast_multiply_fusion, bf16[8,2048,128]{2,0,1:T(8,128)(2,1)} %get-tuple-element.9), kind=kOutput, calls=%fused_computation.6 | convolution fusion | flops 4294967296 | bytes 41943040 | tf_op jit(solution)/shard_map/fmk,fkp->fmp/dot_general | solution.py:24
  351.7 17.7 %fusion.39 = bf16[1,8,1024,128]{3,2,1,0:T(8,128)(2,1)S(1)} fusion(f32[8,1024,128]{2,1,0:T(8,128)} %fusion.2, bf16[8,2048,128]{2,0,1:T(8,128)(2,1)} %get-tuple-element.9, bf16[2,8,1024,2048]{3,2,1,0:T(8,128)(2,1)} %broadcast_multiply_fusion), kind=kOutput, calls=%fused_computation.58 | convolution fusion | flops 4297064448 | bytes 44040192 | tf_op jit(solution)/shard_map/fmk,fkp->fmp/dot_general | solution.py:33
  369.4 17.5 %fusion.38 = bf16[1,8,1024,128]{3,2,1,0:T(8,128)(2,1)} fusion(f32[8,1024,128]{2,1,0:T(8,128)} %fusion.3, bf16[8,2048,128]{2,0,1:T(8,128)(2,1)S(1)} %copy-done.6, bf16[2,8,1024,2048]{3,2,1,0:T(8,128)(2,1)} %broadcast_multiply_fusion), kind=kOutput, calls=%fused_computation.57 | convolution fusion | flops 4297064448 | bytes 44040192 | tf_op jit(solution)/shard_map/fmk,fkp->fmp/dot_general | solution.py:27
  391.6 98.8 %all_to_all.36 = bf16[2,8,1024,128]{3,1,0,2:T(8,128)(2,1)S(1)} all-to-all(bf16[2,8,1024,128]{3,1,0,2:T(8,128)(2,1)S(1)} %copy.41), channel_id=1, replica_groups=mesh['freq'=16,'rows'=2] {'freq'}, dimensions={2} | all-to-all | bytes 8388608 | tf_op jit(solution)/shard_map/all_to_all | solution.py:45
  491.6 17.6 %fusion.22 = f32[64,128,512,1]{2,1,3,0:T(8,128)} fusion(bf16[2,128,64,128]{3,2,1,0:T(8,128)(2,1)S(1)} %bitcast.85, f32[1,128,512]{2,1,0:T(8,128)S(1)} %copy-done.4, f32[1,128,512]{2,1,0:T(8,128)S(1)} %copy-done.2), kind=kOutput, calls=%fused_computation.41 | convolution fusion | flops 12885164032 | bytes 21495808 | tf_op jit(solution)/shard_map/kjrp,kjt->rpt/dot_general | solution.py:46
  509.2 18.9 %fusion.35 = bf16[2,128,64,128]{3,1,2,0:T(8,128)(2,1)S(1)} fusion(f32[64,128,512]{2,1,0:T(8,128)S(1)} %bitcast.84, f32[64,128,512,1]{2,1,3,0:T(8,128)} %fusion.22, s32[64,128]{1,0:T(8,128)S(1)} %copy-done.7, f32[1,128,512]{2,1,0:T(8,128)S(1)} %copy-done.4, f32[1,128,512]{2,1,0:T(8,128)S(1)} %copy-done.2), kind=kOutput, calls=%fused_computation.56 | convolution fusion | flops 12899844096 | bytes 38305792 | tf_op jit(solution)/shard_map/rpt,kjt->kjrp/dot_general | solution.py:53
  553.1 30.6 %collective-permute-start.23 = (bf16[2,8,64,128]{3,1,2,0:T(8,128)(2,1)S(1)}, bf16[2,8,64,128]{3,1,2,0:T(8,128)(2,1)S(1)}, u32[]{:S(2)}, u32[]{:S(2)}) collective-permute-start(bf16[2,8,64,128]{3,1,2,0:T(8,128)(2,1)S(1)} %get-tuple-element.17), channel_id=1, source_target_pairs={{0,14},{2,16},{4,18},{6,20},{8,22},{10,24},{12,26},{14,28},{16,30}... | collective-permute-start | bytes 786440 | tf_op jit(solution)/shard_map/ppermute | solution.py:65
  583.9 28.3 %collective-permute-done.21 = bf16[2,8,64,128]{3,1,2,0:T(8,128)(2,1)S(1)} collective-permute-done((bf16[2,8,64,128]{3,1,2,0:T(8,128)(2,1)S(1)}, bf16[2,8,64,128]{3,1,2,0:T(8,128)(2,1)S(1)}, u32[]{:S(2)}, u32[]{:S(2)}) %collective-permute-start.21) | collective-permute-done | bytes 262176 | tf_op jit(solution)/shard_map/ppermute | solution.py:65
  624.8 16.1 %fusion.17 = bf16[2,8,1024,128]{3,1,2,0:T(8,128)(2,1)} fusion(s32[]{:T(128)S(6)} %select_n.53, bf16[2,8,1024,128]{3,1,2,0:T(8,128)(2,1)S(1)} %slice_dynamic-update-slice_fusion), kind=kLoop, calls=%fused_computation.30 | loop fusion | flops 2097152 | bytes 8388612 | tf_op jit(solution)/shard_map/jit(_roll_dynamic)/concatenate | solution.py:70
  640.9 111.0 %all-gather.5.cloned.1.call-done = bf16[2,8,2048,128]{3,1,2,0:T(8,128)(2,1)} async-done(((bf16[2,8,1024,128]{3,1,2,0:T(8,128)(2,1)}), bf16[2,8,2048,128]{3,1,2,0:T(8,128)(2,1)}) %all-gather.5.cloned.1.call-update) | async-done | bytes 8388624 | tf_op jit(solution)/shard_map/all_gather | solution.py:40
  757.9 17.6 %fusion = f32[8,1024,128]{2,1,0:T(8,128)} fusion(bf16[2,8,1024,2048]{3,2,1,0:T(8,128)(2,1)} %broadcast_multiply_fusion, bf16[8,2048,128]{2,0,1:T(8,128)(2,1)} %get-tuple-element.8), kind=kOutput, calls=%fused_computation.3 | convolution fusion | flops 4294967296 | bytes 41943040 | tf_op jit(solution)/shard_map/fmk,fkp->fmp/dot_general | solution.py:30
  775.4 18.0 %fusion.1 = f32[8,1024,128]{2,1,0:T(8,128)} fusion(bf16[2,8,1024,2048]{3,2,1,0:T(8,128)(2,1)} %broadcast_multiply_fusion, bf16[8,2048,128]{2,0,1:T(8,128)(2,1)} %get-tuple-element.6), kind=kOutput, calls=%fused_computation.4 | convolution fusion | flops 4294967296 | bytes 41943040 | tf_op jit(solution)/shard_map/fmk,fkp->fmp/dot_general | solution.py:24
  793.4 17.7 %fusion.41 = bf16[1,8,1024,128]{3,2,1,0:T(8,128)(2,1)S(1)} fusion(f32[8,1024,128]{2,1,0:T(8,128)} %fusion, bf16[8,2048,128]{2,0,1:T(8,128)(2,1)} %get-tuple-element.6, bf16[2,8,1024,2048]{3,2,1,0:T(8,128)(2,1)} %broadcast_multiply_fusion), kind=kOutput, calls=%fused_computation.60 | convolution fusion | flops 4297064448 | bytes 44040192 | tf_op jit(solution)/shard_map/fmk,fkp->fmp/dot_general | solution.py:33
  811.1 17.3 %fusion.40 = bf16[1,8,1024,128]{3,2,1,0:T(8,128)(2,1)} fusion(f32[8,1024,128]{2,1,0:T(8,128)} %fusion.1, bf16[8,2048,128]{2,0,1:T(8,128)(2,1)S(1)} %copy-done.5, bf16[2,8,1024,2048]{3,2,1,0:T(8,128)(2,1)} %broadcast_multiply_fusion), kind=kOutput, calls=%fused_computation.59 | convolution fusion | flops 4297064448 | bytes 44040192 | tf_op jit(solution)/shard_map/fmk,fkp->fmp/dot_general | solution.py:27
  833.1 98.8 %all_to_all.37 = bf16[2,8,1024,128]{3,1,0,2:T(8,128)(2,1)S(1)} all-to-all(bf16[2,8,1024,128]{3,1,0,2:T(8,128)(2,1)S(1)} %copy.49), channel_id=1, replica_groups=mesh['freq'=16,'rows'=2] {'freq'}, dimensions={2} | all-to-all | bytes 8388608 | tf_op jit(solution)/shard_map/all_to_all | solution.py:45
  933.0 20.1 %fusion.8 = f32[64,128,512]{2,1,0:T(8,128)} fusion(f32[64,128,512]{2,1,0:T(8,128)} %param.10, s32[64,128]{1,0:T(8,128)S(1)} %copy-done.7, bf16[2,128,64,128]{3,2,1,0:T(8,128)(2,1)S(1)} %bitcast.88, f32[1,128,512]{2,1,0:T(8,128)S(1)} %copy-done.4, f32[1,128,512]{2,1,0:T(8,128)S(1)} %copy-done.2), kind=kOutput, calls=%fused_computation.12 | convolution fusion | flops 12897746944 | bytes 38305792 | tf_op jit(solution)/shard_map/kjrp,kjt->rpt/dot_general | solution.py:46
  (136 shorter events, 122.5 us)
Async XLA Ops:
  6.5 304.1 %all-gather.3.cloned.1.call-start = ((), (), s32[]{:S(2)}) async-start(), calls=%async_computation.2 | async-start | bytes 12582912 | tf_op jit(solution)/shard_map/all_gather | solution.py:40
  30.9 77.7 %collective-permute-start = (bf16[2,8,64,128]{3,1,2,0:T(8,128)(2,1)}, bf16[2,8,64,128]{3,1,2,0:T(8,128)(2,1)}, u32[]{:S(2)}, u32[]{:S(2)}) collective-permute-start(bf16[2,8,64,128]{3,1,2,0:T(8,128)(2,1)} %get-tuple-element.40), channel_id=1, source_target_pairs={{0,30},{2,0},{4,2},{6,4},{8,6},{10,8},{12,10},{14,12},{16,14},{18,... | collective-permute-start | bytes 786440 | tf_op jit(solution)/shard_map/ppermute | solution.py:65
  31.0 81.3 %collective-permute-start.1 = (bf16[2,8,64,128]{3,1,2,0:T(8,128)(2,1)}, bf16[2,8,64,128]{3,1,2,0:T(8,128)(2,1)}, u32[]{:S(2)}, u32[]{:S(2)}) collective-permute-start(bf16[2,8,64,128]{3,1,2,0:T(8,128)(2,1)} %get-tuple-element.39), channel_id=1, source_target_pairs={{0,28},{2,30},{4,0},{6,2},{8,4},{10,6},{12,8},{14,10},{16,12},{18,... | collective-permute-start | bytes 786440 | tf_op jit(solution)/shard_map/ppermute | solution.py:65
  36.7 77.6 %collective-permute-start.2 = (bf16[2,8,64,128]{3,1,2,0:T(8,128)(2,1)S(1)}, bf16[2,8,64,128]{3,1,2,0:T(8,128)(2,1)}, u32[]{:S(2)}, u32[]{:S(2)}) collective-permute-start(bf16[2,8,64,128]{3,1,2,0:T(8,128)(2,1)S(1)} %get-tuple-element.38), channel_id=1, source_target_pairs={{0,26},{2,28},{4,30},{6,0},{8,2},{10,4},{12,6},{14,8},{16,10},{18,... | collective-permute-start | bytes 786440 | tf_op jit(solution)/shard_map/ppermute | solution.py:65
  37.9 81.1 %collective-permute-start.3 = (bf16[2,8,64,128]{3,1,2,0:T(8,128)(2,1)S(1)}, bf16[2,8,64,128]{3,1,2,0:T(8,128)(2,1)}, u32[]{:S(2)}, u32[]{:S(2)}) collective-permute-start(bf16[2,8,64,128]{3,1,2,0:T(8,128)(2,1)S(1)} %get-tuple-element.37), channel_id=1, source_target_pairs={{0,24},{2,26},{4,28},{6,30},{8,0},{10,2},{12,4},{14,6},{16,8},{18,... | collective-permute-start | bytes 786440 | tf_op jit(solution)/shard_map/ppermute | solution.py:65
  38.1 82.0 %collective-permute-start.4 = (bf16[2,8,64,128]{3,1,2,0:T(8,128)(2,1)S(1)}, bf16[2,8,64,128]{3,1,2,0:T(8,128)(2,1)}, u32[]{:S(2)}, u32[]{:S(2)}) collective-permute-start(bf16[2,8,64,128]{3,1,2,0:T(8,128)(2,1)S(1)} %get-tuple-element.36), channel_id=1, source_target_pairs={{0,22},{2,24},{4,26},{6,28},{8,30},{10,0},{12,2},{14,4},{16,6},{18... | collective-permute-start | bytes 786440 | tf_op jit(solution)/shard_map/ppermute | solution.py:65
  112.2 46.1 %collective-permute-start.6 = (bf16[2,8,64,128]{3,1,2,0:T(8,128)(2,1)S(1)}, bf16[2,8,64,128]{3,1,2,0:T(8,128)(2,1)S(1)}, u32[]{:S(2)}, u32[]{:S(2)}) collective-permute-start(bf16[2,8,64,128]{3,1,2,0:T(8,128)(2,1)S(1)} %get-tuple-element.34), channel_id=1, source_target_pairs={{0,18},{2,20},{4,22},{6,24},{8,26},{10,28},{12,30},{14,0},{16,2},{... | collective-permute-start | bytes 786440 | tf_op jit(solution)/shard_map/ppermute | solution.py:65
  114.4 53.3 %collective-permute-start.7 = (bf16[2,8,64,128]{3,1,2,0:T(8,128)(2,1)S(1)}, bf16[2,8,64,128]{3,1,2,0:T(8,128)(2,1)S(1)}, u32[]{:S(2)}, u32[]{:S(2)}) collective-permute-start(bf16[2,8,64,128]{3,1,2,0:T(8,128)(2,1)S(1)} %get-tuple-element.33), channel_id=1, source_target_pairs={{0,16},{2,18},{4,20},{6,22},{8,24},{10,26},{12,28},{14,30},{16,0},... | collective-permute-start | bytes 786440 | tf_op jit(solution)/shard_map/ppermute | solution.py:65
  119.1 50.7 %collective-permute-start.8 = (bf16[2,8,64,128]{3,1,2,0:T(8,128)(2,1)S(1)}, bf16[2,8,64,128]{3,1,2,0:T(8,128)(2,1)S(1)}, u32[]{:S(2)}, u32[]{:S(2)}) collective-permute-start(bf16[2,8,64,128]{3,1,2,0:T(8,128)(2,1)S(1)} %get-tuple-element.32), channel_id=1, source_target_pairs={{0,14},{2,16},{4,18},{6,20},{8,22},{10,24},{12,26},{14,28},{16,30}... | collective-permute-start | bytes 786440 | tf_op jit(solution)/shard_map/ppermute | solution.py:65
  120.1 62.8 %collective-permute-start.9 = (bf16[2,8,64,128]{3,1,2,0:T(8,128)(2,1)S(1)}, bf16[2,8,64,128]{3,1,2,0:T(8,128)(2,1)S(1)}, u32[]{:S(2)}, u32[]{:S(2)}) collective-permute-start(bf16[2,8,64,128]{3,1,2,0:T(8,128)(2,1)S(1)} %get-tuple-element.31), channel_id=1, source_target_pairs={{0,12},{2,14},{4,16},{6,18},{8,20},{10,22},{12,24},{14,26},{16,28}... | collective-permute-start | bytes 786440 | tf_op jit(solution)/shard_map/ppermute | solution.py:65
  121.5 61.7 %collective-permute-start.10 = (bf16[2,8,64,128]{3,1,2,0:T(8,128)(2,1)S(1)}, bf16[2,8,64,128]{3,1,2,0:T(8,128)(2,1)S(1)}, u32[]{:S(2)}, u32[]{:S(2)}) collective-permute-start(bf16[2,8,64,128]{3,1,2,0:T(8,128)(2,1)S(1)} %get-tuple-element.30), channel_id=1, source_target_pairs={{0,10},{2,12},{4,14},{6,16},{8,18},{10,20},{12,22},{14,24},{16,26}... | collective-permute-start | bytes 786440 | tf_op jit(solution)/shard_map/ppermute | solution.py:65
  158.3 24.9 %collective-permute-start.11 = (bf16[2,8,64,128]{3,1,2,0:T(8,128)(2,1)S(1)}, bf16[2,8,64,128]{3,1,2,0:T(8,128)(2,1)S(1)}, u32[]{:S(2)}, u32[]{:S(2)}) collective-permute-start(bf16[2,8,64,128]{3,1,2,0:T(8,128)(2,1)S(1)} %get-tuple-element.29), channel_id=1, source_target_pairs={{0,8},{2,10},{4,12},{6,14},{8,16},{10,18},{12,20},{14,22},{16,24},... | collective-permute-start | bytes 786440 | tf_op jit(solution)/shard_map/ppermute | solution.py:65
  167.6 15.7 %collective-permute-start.12 = (bf16[2,8,64,128]{3,1,2,0:T(8,128)(2,1)S(1)}, bf16[2,8,64,128]{3,1,2,0:T(8,128)(2,1)S(1)}, u32[]{:S(2)}, u32[]{:S(2)}) collective-permute-start(bf16[2,8,64,128]{3,1,2,0:T(8,128)(2,1)S(1)} %get-tuple-element.28), channel_id=1, source_target_pairs={{0,6},{2,8},{4,10},{6,12},{8,14},{10,16},{12,18},{14,20},{16,22},{... | collective-permute-start | bytes 786440 | tf_op jit(solution)/shard_map/ppermute | solution.py:65
  169.7 13.6 %collective-permute-start.13 = (bf16[2,8,64,128]{3,1,2,0:T(8,128)(2,1)S(1)}, bf16[2,8,64,128]{3,1,2,0:T(8,128)(2,1)S(1)}, u32[]{:S(2)}, u32[]{:S(2)}) collective-permute-start(bf16[2,8,64,128]{3,1,2,0:T(8,128)(2,1)S(1)} %get-tuple-element.27), channel_id=1, source_target_pairs={{0,4},{2,6},{4,8},{6,10},{8,12},{10,14},{12,16},{14,18},{16,20},{1... | collective-permute-start | bytes 786440 | tf_op jit(solution)/shard_map/ppermute | solution.py:65
  203.4 548.5 %all-gather.5.cloned.1.call-start = ((), (), s32[]{:S(2)}) async-start(), calls=%async_computation.3 | async-start | bytes 12582912 | tf_op jit(solution)/shard_map/all_gather | solution.py:40
  534.8 17.6 %collective-permute-start.17 = (bf16[2,8,64,128]{3,1,2,0:T(8,128)(2,1)S(1)}, bf16[2,8,64,128]{3,1,2,0:T(8,128)(2,1)S(1)}, u32[]{:S(2)}, u32[]{:S(2)}) collective-permute-start(bf16[2,8,64,128]{3,1,2,0:T(8,128)(2,1)S(1)} %get-tuple-element.23), channel_id=1, source_target_pairs={{0,26},{2,28},{4,30},{6,0},{8,2},{10,4},{12,6},{14,8},{16,10},{18,... | collective-permute-start | bytes 786440 | tf_op jit(solution)/shard_map/ppermute | solution.py:65
  535.8 17.2 %collective-permute-start.18 = (bf16[2,8,64,128]{3,1,2,0:T(8,128)(2,1)S(1)}, bf16[2,8,64,128]{3,1,2,0:T(8,128)(2,1)S(1)}, u32[]{:S(2)}, u32[]{:S(2)}) collective-permute-start(bf16[2,8,64,128]{3,1,2,0:T(8,128)(2,1)S(1)} %get-tuple-element.22), channel_id=1, source_target_pairs={{0,24},{2,26},{4,28},{6,30},{8,0},{10,2},{12,4},{14,6},{16,8},{18,... | collective-permute-start | bytes 786440 | tf_op jit(solution)/shard_map/ppermute | solution.py:65
  537.5 46.2 %collective-permute-start.19 = (bf16[2,8,64,128]{3,1,2,0:T(8,128)(2,1)S(1)}, bf16[2,8,64,128]{3,1,2,0:T(8,128)(2,1)S(1)}, u32[]{:S(2)}, u32[]{:S(2)}) collective-permute-start(bf16[2,8,64,128]{3,1,2,0:T(8,128)(2,1)S(1)} %get-tuple-element.21), channel_id=1, source_target_pairs={{0,22},{2,24},{4,26},{6,28},{8,30},{10,0},{12,2},{14,4},{16,6},{18... | collective-permute-start | bytes 786440 | tf_op jit(solution)/shard_map/ppermute | solution.py:65
  540.4 43.4 %collective-permute-start.20 = (bf16[2,8,64,128]{3,1,2,0:T(8,128)(2,1)S(1)}, bf16[2,8,64,128]{3,1,2,0:T(8,128)(2,1)S(1)}, u32[]{:S(2)}, u32[]{:S(2)}) collective-permute-start(bf16[2,8,64,128]{3,1,2,0:T(8,128)(2,1)S(1)} %get-tuple-element.20), channel_id=1, source_target_pairs={{0,20},{2,22},{4,24},{6,26},{8,28},{10,30},{12,0},{14,2},{16,4},{1... | collective-permute-start | bytes 786440 | tf_op jit(solution)/shard_map/ppermute | solution.py:65
  542.7 69.5 %collective-permute-start.21 = (bf16[2,8,64,128]{3,1,2,0:T(8,128)(2,1)S(1)}, bf16[2,8,64,128]{3,1,2,0:T(8,128)(2,1)S(1)}, u32[]{:S(2)}, u32[]{:S(2)}) collective-permute-start(bf16[2,8,64,128]{3,1,2,0:T(8,128)(2,1)S(1)} %get-tuple-element.19), channel_id=1, source_target_pairs={{0,18},{2,20},{4,22},{6,24},{8,26},{10,28},{12,30},{14,0},{16,2},{... | collective-permute-start | bytes 786440 | tf_op jit(solution)/shard_map/ppermute | solution.py:65
  552.4 59.9 %collective-permute-start.22 = (bf16[2,8,64,128]{3,1,2,0:T(8,128)(2,1)S(1)}, bf16[2,8,64,128]{3,1,2,0:T(8,128)(2,1)S(1)}, u32[]{:S(2)}, u32[]{:S(2)}) collective-permute-start(bf16[2,8,64,128]{3,1,2,0:T(8,128)(2,1)S(1)} %get-tuple-element.18), channel_id=1, source_target_pairs={{0,16},{2,18},{4,20},{6,22},{8,24},{10,26},{12,28},{14,30},{16,0},... | collective-permute-start | bytes 786440 | tf_op jit(solution)/shard_map/ppermute | solution.py:65
  553.1 59.4 %collective-permute-start.23 = (bf16[2,8,64,128]{3,1,2,0:T(8,128)(2,1)S(1)}, bf16[2,8,64,128]{3,1,2,0:T(8,128)(2,1)S(1)}, u32[]{:S(2)}, u32[]{:S(2)}) collective-permute-start(bf16[2,8,64,128]{3,1,2,0:T(8,128)(2,1)S(1)} %get-tuple-element.17), channel_id=1, source_target_pairs={{0,14},{2,16},{4,18},{6,20},{8,22},{10,24},{12,26},{14,28},{16,30}... | collective-permute-start | bytes 786440 | tf_op jit(solution)/shard_map/ppermute | solution.py:65
  583.7 28.9 %collective-permute-start.24 = (bf16[2,8,64,128]{3,1,2,0:T(8,128)(2,1)S(1)}, bf16[2,8,64,128]{3,1,2,0:T(8,128)(2,1)S(1)}, u32[]{:S(2)}, u32[]{:S(2)}) collective-permute-start(bf16[2,8,64,128]{3,1,2,0:T(8,128)(2,1)S(1)} %get-tuple-element.16), channel_id=1, source_target_pairs={{0,12},{2,14},{4,16},{6,18},{8,20},{10,22},{12,24},{14,26},{16,28}... | collective-permute-start | bytes 786440 | tf_op jit(solution)/shard_map/ppermute | solution.py:65
  583.8 30.3 %collective-permute-start.25 = (bf16[2,8,64,128]{3,1,2,0:T(8,128)(2,1)S(1)}, bf16[2,8,64,128]{3,1,2,0:T(8,128)(2,1)S(1)}, u32[]{:S(2)}, u32[]{:S(2)}) collective-permute-start(bf16[2,8,64,128]{3,1,2,0:T(8,128)(2,1)S(1)} %get-tuple-element.15), channel_id=1, source_target_pairs={{0,10},{2,12},{4,14},{6,16},{8,18},{10,20},{12,22},{14,24},{16,26}... | collective-permute-start | bytes 786440 | tf_op jit(solution)/shard_map/ppermute | solution.py:65
  (21 other events, 250.1 us)
Sparse Core Ops, SparseCore 0:
  203.5 107.0 all-gather.2
  641.1 110.7 all-gather.4
